TPU v7x, 32 devices: a whole 2x2x4 slice. The times are simulated.
32 devices in a mesh: cell: 8 (over y, x, core), chan: 4 (over z).
Axes of the slice: x: 2, y: 2, z: 4, core: 2. Of those that a mesh axis runs over, the one named last changes fastest.
Arguments:
- embeds: float32 [32768, 512], P('cell', 'chan'), may hold values from -260 to 260
Outputs:
- whitened: float32 [32768, 512], P(('cell', 'chan'))
- factor: float32 [512, 512], replicated
All inputs are finite; a program needn't handle non-finite values.
Results may differ from a plain program's by a relative error of at most 0.000088.
Values sent between devices are 32-bit elements; how exact they have to be, the bound alone decides.
No kernel may reach another device: no remote copies, remote signals or barrier semaphores. Data moves between devices by JAX's collectives and lax.ppermute only.
A program may use at most 64 MiB of HBM per device.

v0:
```python
import math
import jax
import jax.numpy as jnp
from jax import lax
from jax.sharding import PartitionSpec as P


def per_device(embeds):
    rows = lax.all_to_all(embeds, "chan", split_axis=0, concat_axis=1, tiled=True)
    partial_value = lax.dot_general(
        rows,
        rows,
        (((0,), (0,)), ((), ())),
        precision=lax.Precision.HIGHEST,
        preferred_element_type=jnp.float32,
    )
    within = lax.psum(partial_value, "cell")
    gram = lax.psum(within, "chan")
    lower = jnp.linalg.cholesky(gram)
    upper = lower.T
    total = rows.shape[0] * lax.axis_size("cell") * lax.axis_size("chan")
    scale = math.sqrt(total)
    whitened = jax.scipy.linalg.solve_triangular(lower, rows.T, lower=True).T * scale
    return (whitened, upper / scale)


def solution(mesh):
    in_specs = (P("cell", "chan"),)
    out_specs = (P(("cell", "chan"), None), P())
    return jax.shard_map(
        per_device, mesh=mesh, in_specs=in_specs, out_specs=out_specs, check_vma=False
    )
```

profile of v0, /device:TPU:0, one launch (start us, length us, event | category | flops | bytes accessed | tf_op | source)
XLA Modules:
  0.0 345.4 jit_solution(12368861745308110171)
XLA Ops:
  7.2 54.7 %all_to_all.19 = f32[4,1024,128]{2,1,0:T(8,128)} all-to-all(f32[4,1024,128]{2,1,0:T(8,128)} %bitcast.65), channel_id=1, replica_groups=mesh['cell'=8,'chan'=4] {'chan'}, dimensions={0} | all-to-all | bytes 4194304 | tf_op jit(solution)/shard_map/all_to_all | solution.py:9
  61.9 1.9 copy.11
  63.8 4.5 %fusion.37 = f32[512,512]{0,1:T(8,128)} fusion(f32[1024,512]{0,1:T(8,128)S(1)} %bitcast.59), kind=kOutput, calls=%fused_computation.71 | convolution fusion | flops 3221225472 | bytes 3145728 | tf_op jit(solution)/shard_map/dot_general | solution.py:10
  68.8 55.6 %all-reduce.4.cloned.1.call-done = f32[512,512]{0,1:T(8,128)} async-done(((f32[512,512]{0,1:T(8,128)}), f32[512,512]{0,1:T(8,128)}) %all-reduce.4.cloned.1.call-update) | async-done | bytes 1048592 | tf_op jit(solution)/shard_map/psum | solution.py:17
  124.4 53.5 %all-reduce.6.cloned.1.call-done = f32[512,512]{0,1:T(8,128)} async-done(((f32[512,512]{0,1:T(8,128)}), f32[512,512]{0,1:T(8,128)}) %all-reduce.6.cloned.1.call-update) | async-done | bytes 1048592 | tf_op jit(solution)/shard_map/psum | solution.py:18
  177.9 2.6 copy.13
  183.0 11.7 %cholesky.104 = f32[128,128]{1,0:T(8,128)S(1)} custom-call(f32[128,128]{1,0:T(8,128)S(1)} %cholesky.266), custom_call_target="Cholesky" | custom-call | tf_op jit(solution)/shard_map/jit(cholesky)/cholesky | solution.py:19
  194.7 9.8 %custom-call.31 = f32[1,128,128]{1,2,0:T(8,128)S(1)} custom-call(f32[1,128,128]{2,1,0:T(8,128)S(1)} %get-tuple-element.37), custom_call_target="InvertDiagBlocksLowerTriangular" | custom-call | tf_op jit(solution)/shard_map/jit(cholesky)/cholesky | solution.py:19
  207.2 11.7 %cholesky.217 = f32[128,128]{1,0:T(8,128)S(1)} custom-call(f32[128,128]{1,0:T(8,128)S(1)} %cholesky.270), custom_call_target="Cholesky" | custom-call | tf_op jit(solution)/shard_map/jit(cholesky)/cholesky | solution.py:19
  218.9 9.9 %custom-call.32 = f32[1,128,128]{1,2,0:T(8,128)S(1)} custom-call(f32[1,128,128]{2,1,0:T(8,128)S(1)} %get-tuple-element.34), custom_call_target="InvertDiagBlocksLowerTriangular" | custom-call | tf_op jit(solution)/shard_map/jit(cholesky)/cholesky | solution.py:19
  230.4 11.7 %cholesky.238 = f32[128,128]{1,0:T(8,128)S(1)} custom-call(f32[128,128]{1,0:T(8,128)S(1)} %cholesky.275), custom_call_target="Cholesky" | custom-call | tf_op jit(solution)/shard_map/jit(cholesky)/cholesky | solution.py:19
  242.9 9.8 %custom-call.33 = f32[1,128,128]{1,2,0:T(8,128)S(1)} custom-call(f32[1,128,128]{2,1,0:T(8,128)S(1)} %get-tuple-element.31), custom_call_target="InvertDiagBlocksLowerTriangular" | custom-call | tf_op jit(solution)/shard_map/jit(cholesky)/cholesky | solution.py:19
  254.2 11.7 %cholesky.255 = f32[128,128]{1,0:T(8,128)S(1)} custom-call(f32[128,128]{1,0:T(8,128)S(1)} %convolution_subtract_fusion.4), custom_call_target="Cholesky" | custom-call | tf_op jit(solution)/shard_map/jit(cholesky)/cholesky | solution.py:19
  269.7 1.8 multiply_bitcast_fusion
  271.5 2.5 copy.15
  274.1 14.4 %while.1 = (s32[]{:T(128)}, f32[512,512]{1,0:T(8,128)}, s32[4,2]{0,1:T(2,128)S(1)}, f32[4,128,128]{2,1,0:T(8,128)}, s32[]{:T(128)}) while((s32[]{:T(128)}, f32[512,512]{1,0:T(8,128)}, s32[4,2]{0,1:T(2,128)S(1)}, f32[4,128,128]{2,1,0:T(8,128)}, s32[]{:T(128)}) %tuple.35), condition=%wide.while_cond, body=%wide.while_body.sunk | while | flops 2 | bytes 132205 | solution.py:23
  274.7 3.0 bitcast_dynamic-update-slice_fusion.2
  278.4 3.0 bitcast_dynamic-update-slice_fusion.2
  282.0 3.0 bitcast_dynamic-update-slice_fusion.2
  285.6 2.9 bitcast_dynamic-update-slice_fusion.2
  288.5 40.1 %custom-call.34 = f32[4,128,128]{1,2,0:T(8,128)S(1)} custom-call(f32[4,128,128]{2,1,0:T(8,128)} %get-tuple-element.9), custom_call_target="InvertDiagBlocksLowerTriangular" | custom-call | tf_op jit(solution)/shard_map/jit(_solve_triangular)/triangular_solve | solution.py:23
  331.3 1.6 convolution_subtract_fusion
  333.6 2.0 fusion.7
  336.5 1.8 copy.14
  (43 shorter events, 17.6 us)
Async XLA Ops:
  7.2 117.2 %all-reduce.4.cloned.1.call-start = ((), (), s32[]{:S(2)}) async-start(), calls=%async_computation.1 | async-start | bytes 2097152 | tf_op jit(solution)/shard_map/psum | solution.py:17
  68.3 109.6 %all-reduce.6.cloned.1.call-start = ((), (), s32[]{:S(2)}) async-start(), calls=%async_computation.2 | async-start | bytes 2097152 | tf_op jit(solution)/shard_map/psum | solution.py:18
  177.9 2.6 copy-start
  182.0 1.0 copy-start.1
Sparse Core Ops, SparseCore 0:
  68.4 55.9 all-reduce.3
  126.7 51.1 all-reduce.5
where the time goes:
time: 350 us; the launch traced here: 345 us
  other arithmetic  122 us (35%)
  waiting for transfers between devices  109 us (31%)
  blocking collectives  54.7 us (16%)
  local copies, waits for them, and re-layouts  24.4 us (7%)
  matrix products  17.5 us (5%)
  between operations  17 us (5%)
    another operation x14, other arithmetic, per_device(): lower = jnp.linalg.cholesky(gram)  78.5 us
    psum x1, waiting for transfers between devices, per_device(): within = lax.psum(partial_value, 'cell')  55.6 us
    all_to_all x1, blocking collectives, per_device(): lax.all_to_all(embeds, 'chan', split_axis=0, concat_axis=1, tiled=True)  54.7 us
    psum x1, waiting for transfers between devices, per_device(): gram = lax.psum(within, 'chan')  53.5 us
    another operation x2, other arithmetic, per_device(): jax.scipy.linalg.solve_triangular(lower, rows.T, lower=True).T * scale  40.1 us
    another operation x12, local copies, waits for them, and re-layouts  14.4 us
    another operation x7, matrix products, per_device(): jax.scipy.linalg.solve_triangular(lower, rows.T, lower=True).T * scale  7.6 us
  transfers between devices with their start and end apart: 2, of which 2 were waited for; matrix products, arithmetic and copies ran while one was open for 0% of the time, Pallas kernels for 0%

commit v1 on v0

--- a/solution.py
+++ b/solution.py
@@ -6,7 +6,9 @@
 
 
 def per_device(embeds):
-    rows = lax.all_to_all(embeds, "chan", split_axis=0, concat_axis=1, tiled=True)
+    pieces = jnp.split(embeds, lax.axis_size("chan"), axis=0)
+    received = lax.all_to_all(jnp.stack(pieces), "chan", 0, 0)
+    rows = jnp.concatenate(received, axis=1)
     partial_value = lax.dot_general(
         rows,
         rows,

time: 350 us -> 351 us (level)
  no operation moved by 1% of the time
where the time goes in v1:
time: 351 us; the launch traced here: 346 us
  other arithmetic  122 us (35%)
  waiting for transfers between devices  109 us (31%)
  blocking collectives  54.3 us (15%)
  local copies, waits for them, and re-layouts  24.9 us (7%)
  matrix products  17.5 us (5%)
  between operations  17 us (5%)
    another operation x14, other arithmetic, per_device(): lower = jnp.linalg.cholesky(gram)  78.5 us
    psum x1, waiting for transfers between devices, per_device(): within = lax.psum(partial_value, 'cell')  55.6 us
    all_to_all x1, blocking collectives, per_device(): received = lax.all_to_all(jnp.stack(pieces), 'chan', 0, 0)  54.3 us
    psum x1, waiting for transfers between devices, per_device(): gram = lax.psum(within, 'chan')  53.5 us
    another operation x2, other arithmetic, per_device(): jax.scipy.linalg.solve_triangular(lower, rows.T, lower=True).T * scale  40.1 us
    another operation x12, local copies, waits for them, and re-layouts  14.4 us
    another operation x7, matrix products, per_device(): jax.scipy.linalg.solve_triangular(lower, rows.T, lower=True).T * scale  7.6 us
  transfers between devices with their start and end apart: 2, of which 2 were waited for; matrix products, arithmetic and copies ran while one was open for 0% of the time, Pallas kernels for 0%

profile of v1, /device:TPU:0, one launch (start us, length us, event | category | flops | bytes accessed | tf_op | source)
XLA Modules:
  0.0 345.8 jit_solution(10953714847248413214)
XLA Ops:
  7.2 1.7 fusion.37
  9.8 54.3 %all_to_all.5 = f32[4,1024,128]{1,2,0:T(8,128)S(1)} all-to-all(f32[4,1024,128]{1,2,0:T(8,128)S(1)} %pad_maximum_fusion), channel_id=1, replica_groups=mesh['cell'=8,'chan'=4] {'chan'}, dimensions={0} | all-to-all | bytes 4194304 | tf_op jit(solution)/shard_map/all_to_all | solution.py:10
  64.2 4.5 %fusion.38 = f32[512,512]{0,1:T(8,128)} fusion(f32[1024,512]{0,1:T(8,128)S(1)} %bitcast.63), kind=kOutput, calls=%fused_computation.73 | convolution fusion | flops 3221225472 | bytes 3145728 | tf_op jit(solution)/shard_map/dot_general | solution.py:12
  69.2 55.6 %all-reduce.4.cloned.1.call-done = f32[512,512]{0,1:T(8,128)} async-done(((f32[512,512]{0,1:T(8,128)}), f32[512,512]{0,1:T(8,128)}) %all-reduce.4.cloned.1.call-update) | async-done | bytes 1048592 | tf_op jit(solution)/shard_map/psum | solution.py:19
  124.8 53.5 %all-reduce.6.cloned.1.call-done = f32[512,512]{0,1:T(8,128)} async-done(((f32[512,512]{0,1:T(8,128)}), f32[512,512]{0,1:T(8,128)}) %all-reduce.6.cloned.1.call-update) | async-done | bytes 1048592 | tf_op jit(solution)/shard_map/psum | solution.py:20
  178.3 2.6 copy.12
  183.4 11.7 %cholesky.104 = f32[128,128]{1,0:T(8,128)S(1)} custom-call(f32[128,128]{1,0:T(8,128)S(1)} %cholesky.266), custom_call_target="Cholesky" | custom-call | tf_op jit(solution)/shard_map/jit(cholesky)/cholesky | solution.py:21
  195.1 9.8 %custom-call.31 = f32[1,128,128]{1,2,0:T(8,128)S(1)} custom-call(f32[1,128,128]{2,1,0:T(8,128)S(1)} %get-tuple-element.39), custom_call_target="InvertDiagBlocksLowerTriangular" | custom-call | tf_op jit(solution)/shard_map/jit(cholesky)/cholesky | solution.py:21
  207.6 11.7 %cholesky.217 = f32[128,128]{1,0:T(8,128)S(1)} custom-call(f32[128,128]{1,0:T(8,128)S(1)} %cholesky.270), custom_call_target="Cholesky" | custom-call | tf_op jit(solution)/shard_map/jit(cholesky)/cholesky | solution.py:21
  219.3 9.9 %custom-call.32 = f32[1,128,128]{1,2,0:T(8,128)S(1)} custom-call(f32[1,128,128]{2,1,0:T(8,128)S(1)} %get-tuple-element.36), custom_call_target="InvertDiagBlocksLowerTriangular" | custom-call | tf_op jit(solution)/shard_map/jit(cholesky)/cholesky | solution.py:21
  230.8 11.7 %cholesky.238 = f32[128,128]{1,0:T(8,128)S(1)} custom-call(f32[128,128]{1,0:T(8,128)S(1)} %cholesky.275), custom_call_target="Cholesky" | custom-call | tf_op jit(solution)/shard_map/jit(cholesky)/cholesky | solution.py:21
  243.3 9.8 %custom-call.33 = f32[1,128,128]{1,2,0:T(8,128)S(1)} custom-call(f32[1,128,128]{2,1,0:T(8,128)S(1)} %get-tuple-element.33), custom_call_target="InvertDiagBlocksLowerTriangular" | custom-call | tf_op jit(solution)/shard_map/jit(cholesky)/cholesky | solution.py:21
  254.6 11.7 %cholesky.255 = f32[128,128]{1,0:T(8,128)S(1)} custom-call(f32[128,128]{1,0:T(8,128)S(1)} %convolution_subtract_fusion.4), custom_call_target="Cholesky" | custom-call | tf_op jit(solution)/shard_map/jit(cholesky)/cholesky | solution.py:21
  270.1 1.8 multiply_bitcast_fusion
  271.9 2.5 copy.14
  274.5 14.4 %while.1 = (s32[]{:T(128)}, f32[512,512]{1,0:T(8,128)}, s32[4,2]{0,1:T(2,128)S(1)}, f32[4,128,128]{2,1,0:T(8,128)}, s32[]{:T(128)}) while((s32[]{:T(128)}, f32[512,512]{1,0:T(8,128)}, s32[4,2]{0,1:T(2,128)S(1)}, f32[4,128,128]{2,1,0:T(8,128)}, s32[]{:T(128)}) %tuple.37), condition=%wide.while_cond, body=%wide.while_body.sunk | while | flops 2 | bytes 132205 | solution.py:25
  275.1 3.0 bitcast_dynamic-update-slice_fusion.2
  278.8 3.0 bitcast_dynamic-update-slice_fusion.2
  282.4 3.0 bitcast_dynamic-update-slice_fusion.2
  286.0 2.9 bitcast_dynamic-update-slice_fusion.2
  288.9 40.1 %custom-call.34 = f32[4,128,128]{1,2,0:T(8,128)S(1)} custom-call(f32[4,128,128]{2,1,0:T(8,128)} %get-tuple-element.9), custom_call_target="InvertDiagBlocksLowerTriangular" | custom-call | tf_op jit(solution)/shard_map/jit(_solve_triangular)/triangular_solve | solution.py:25
  331.7 1.6 convolution_subtract_fusion
  334.0 2.0 fusion.7
  336.9 1.8 copy.13
  (48 shorter events, 18.5 us)
Async XLA Ops:
  7.2 117.6 %all-reduce.4.cloned.1.call-start = ((), (), s32[]{:S(2)}) async-start(), calls=%async_computation.1 | async-start | bytes 2097152 | tf_op jit(solution)/shard_map/psum | solution.py:19
  68.7 109.6 %all-reduce.6.cloned.1.call-start = ((), (), s32[]{:S(2)}) async-start(), calls=%async_computation.2 | async-start | bytes 2097152 | tf_op jit(solution)/shard_map/psum | solution.py:20
  178.3 2.6 copy-start
  182.4 1.0 copy-start.1
Sparse Core Ops, SparseCore 0:
  68.8 55.9 all-reduce.3
  127.1 51.1 all-reduce.5
